TPU v7x, 32 devices: a whole 2x2x4 slice. The times are simulated.
32 devices in a mesh: rows: 8 (over y, x, core), cols: 4 (over z).
Axes of the slice: x: 2, y: 2, z: 4, core: 2. Of those that a mesh axis runs over, the one named last changes fastest.
Arguments:
- up_a: bfloat16 [28672, 4096], P('rows', 'cols'), may hold values from -6 to 6
- gate_a: bfloat16 [28672, 4096], P('rows', 'cols'), may hold values from -6 to 6
- down_a: bfloat16 [28672, 4096], P('rows', 'cols'), may hold values from -6 to 6
- up_b: bfloat16 [28672, 4096], P('rows', 'cols'), may hold values from -6 to 6
- gate_b: bfloat16 [28672, 4096], P('rows', 'cols'), may hold values from -6 to 6
- down_b: bfloat16 [28672, 4096], P('rows', 'cols'), may hold values from -6 to 6
- perm: int32 [28672], P('rows'), may hold values from 0 to 28671, as said below
Outputs:
- costs: float32 [28672, 256], P('rows', 'cols')
- up_mean: bfloat16 [28672, 4096], P('rows', 'cols')
- gate_mean: bfloat16 [28672, 4096], P('rows', 'cols')
- down_mean: bfloat16 [28672, 4096], P('rows', 'cols')
Inputs may be any that keep to these rules, and one draw needn't show every extreme that they name: perm is a permutation of the hidden units. Split positions and values alike into aligned blocks of 3584: the positions of one block take at most 448 values from any one block, and exactly 448 from some block.
All inputs are finite; a program needn't handle non-finite values.
Results may differ from a plain program's by a relative error of at most 0.001.
Values may be sent and summed in bfloat16 or wider, within the bound.
A program may use at most 192 MiB of HBM per device.

v0:
```python
import jax
import jax.numpy as jnp
from jax import lax
from jax.sharding import PartitionSpec as P

D = 4096
A_DEV = 32


def local(up_a, gate_a, down_a, up_b, gate_b, down_b, perm):
    row_count = up_a.shape[0]
    features = up_a.shape[1]
    stride = row_count // A_DEV
    cost_scale = (2.0 * D) ** (-0.5)
    window = jnp.stack([up_a[::stride], gate_a[::stride]])
    pieces = lax.all_gather(window[:, None], "rows", axis=1, tiled=True)
    part_up = jnp.einsum("jd,bsd->jsb", up_b, pieces[0], preferred_element_type=jnp.float32)
    part_gate = jnp.einsum("jd,bsd->jsb", gate_b, pieces[1], preferred_element_type=jnp.float32)
    partial_value = part_up + part_gate
    partial_value = partial_value.reshape(row_count, -1)
    costs_out = (
        lax.psum_scatter(partial_value, "cols", scatter_dimension=1, tiled=True) * cost_scale
    )
    peers = lax.axis_size("rows")
    capacity = max(2, (row_count + peers - 1) // peers)
    source = perm // row_count
    local_row = perm % row_count
    matches = (source[:, None] == jnp.arange(peers, dtype=jnp.int32)[None, :]).astype(jnp.int32)
    arrival_rank = jnp.sum(jnp.cumsum(matches, axis=0) * matches, axis=1) - 1
    slot_index = source * capacity + arrival_rank
    wanted = jnp.zeros((peers, capacity), jnp.int32).at[source, arrival_rank].set(local_row)
    asked_rows = lax.all_to_all(wanted, "rows", split_axis=0, concat_axis=0, tiled=True)
    arrived = (
        lax.all_to_all(up_b[asked_rows], "rows", split_axis=0, concat_axis=0, tiled=True),
        lax.all_to_all(gate_b[asked_rows], "rows", split_axis=0, concat_axis=0, tiled=True),
        lax.all_to_all(down_b[asked_rows], "rows", split_axis=0, concat_axis=0, tiled=True),
    )
    mixed = []
    for initial, moved in zip((up_a, gate_a, down_a), arrived):
        flat_rows = moved.reshape(peers * capacity, features)
        picked = jnp.take(flat_rows, slot_index, axis=0)
        mixed.append(
            ((initial.astype(jnp.float32) + picked.astype(jnp.float32)) * 0.5).astype(jnp.bfloat16)
        )
    return (costs_out, mixed[0], mixed[1], mixed[2])


def solution(mesh):
    placed = (
        P("rows", "cols"),
        P("rows", "cols"),
        P("rows", "cols"),
        P("rows", "cols"),
        P("rows", "cols"),
        P("rows", "cols"),
        P("rows"),
    )
    return jax.shard_map(
        local,
        mesh=mesh,
        in_specs=placed,
        out_specs=(P("rows", "cols"), P("rows", "cols"), P("rows", "cols"), P("rows", "cols")),
        check_vma=False,
    )
```

profile of v0, /device:TPU:11, one launch (start us, length us, event | category | flops | bytes accessed | tf_op | source)
XLA Modules:
  0.0 376.3 jit_solution(4634352056040756477)
XLA Ops:
  7.2 0.7 add_select_fusion
  7.9 2.3 reduce-window.6
  10.2 0.3 slice_reduce_fusion
  10.6 0.2 reduce-window.9
  10.7 0.1 add_bitcast_fusion
  10.8 0.1 fusion.12
  11.0 0.8 multiply_reduce_fusion
  11.8 0.8 and_reduce_fusion
  12.6 13.7 %scatter_custom_fusion = s32[3584]{0:T(1024)S(1)} fusion(s32[3584]{0:T(1024)S(1)} %broadcast_select_fusion, s32[3584]{0:T(1024)S(1)} %get-tuple-element.9, s32[]{:T(128)} %constant.26.clone.1), kind=kCustom, calls=%fused_computation.43 | custom fusion | bytes 14340
  26.3 0.1 all_to_all.17
  26.3 7.6 %all_to_all.27 = s32[8,1,448]{2,1,0:T(1,128)S(1)} all-to-all(s32[8,1,448]{2,1,0:T(1,128)S(1)} %all_to_all.17), channel_id=1, replica_groups=mesh['rows'=8,'cols'=4] {'rows'}, dimensions={0} | all-to-all | bytes 28672 | tf_op jit(solution)/shard_map/all_to_all | solution.py:32
  34.1 20.4 %gather_fusion = bf16[3584,1024]{1,0:T(8,128)(2,1)} fusion(bf16[3584,1024]{1,0:T(8,128)(2,1)} %param.12, s32[4096]{0:T(1024)S(1)} %pad_clamp_fusion.1), kind=kCustom, calls=%fused_computation.3 | custom fusion | bytes 14694400 | tf_op jit(solution)/shard_map/gather | solution.py:34
  54.5 6.2 %all-to-all-start.1 = ((bf16[8,448,1024]{2,1,0:T(8,128)(2,1)}), bf16[8,448,1024]{2,1,0:T(8,128)(2,1)}, u32[]{:S(2)}, u32[]{:S(2)}) async-start(bf16[8,448,1024]{2,1,0:T(8,128)(2,1)} %bitcast.50), calls=%async_computation.2 | async-start | bytes 14680064 | tf_op jit(solution)/shard_map/all_to_all | solution.py:34
  60.7 20.4 %gather_fusion.1 = bf16[3584,1024]{1,0:T(8,128)(2,1)} fusion(bf16[3584,1024]{1,0:T(8,128)(2,1)} %param.13, s32[4096]{0:T(1024)S(1)} %pad_clamp_fusion.1), kind=kCustom, calls=%fused_computation.4 | custom fusion | bytes 14694400 | tf_op jit(solution)/shard_map/gather | solution.py:35
  81.1 60.9 %all-to-all-done.1 = bf16[8,448,1024]{2,1,0:T(8,128)(2,1)} async-done(((bf16[8,448,1024]{2,1,0:T(8,128)(2,1)}), bf16[8,448,1024]{2,1,0:T(8,128)(2,1)}, u32[]{:S(2)}, u32[]{:S(2)}) %all-to-all-start.1) | async-done | bytes 7340064 | tf_op jit(solution)/shard_map/all_to_all | solution.py:34
  142.1 6.3 %all-to-all-start.2 = ((bf16[8,448,1024]{2,1,0:T(8,128)(2,1)}), bf16[8,448,1024]{2,1,0:T(8,128)(2,1)}, u32[]{:S(2)}, u32[]{:S(2)}) async-start(bf16[8,448,1024]{2,1,0:T(8,128)(2,1)} %bitcast.49), calls=%async_computation.3 | async-start | bytes 14680064 | tf_op jit(solution)/shard_map/all_to_all | solution.py:35
  148.4 3.2 slice.18
  151.6 3.2 slice.19
  154.8 0.7 pad_maximum_fusion
  155.5 20.4 %gather_fusion.2 = bf16[3584,1024]{1,0:T(8,128)(2,1)} fusion(bf16[3584,1024]{1,0:T(8,128)(2,1)} %param.14, s32[4096]{0:T(1024)S(1)} %pad_clamp_fusion.1), kind=kCustom, calls=%fused_computation.5 | custom fusion | bytes 14694400 | tf_op jit(solution)/shard_map/gather | solution.py:36
  175.9 58.1 %all-to-all-done.2 = bf16[8,448,1024]{2,1,0:T(8,128)(2,1)} async-done(((bf16[8,448,1024]{2,1,0:T(8,128)(2,1)}), bf16[8,448,1024]{2,1,0:T(8,128)(2,1)}, u32[]{:S(2)}, u32[]{:S(2)}) %all-to-all-start.2) | async-done | bytes 7340064 | tf_op jit(solution)/shard_map/all_to_all | solution.py:35
  233.9 6.3 %all-to-all-start.3 = ((bf16[8,448,1024]{2,1,0:T(8,128)(2,1)}), bf16[8,448,1024]{2,1,0:T(8,128)(2,1)}, u32[]{:S(2)}, u32[]{:S(2)}) async-start(bf16[8,448,1024]{2,1,0:T(8,128)(2,1)} %bitcast.48), calls=%async_computation.4 | async-start | bytes 14680064 | tf_op jit(solution)/shard_map/all_to_all | solution.py:36
  240.3 1.4 fusion.18
  241.7 5.4 %fusion = f32[8,32,3584]{2,1,0:T(8,128)S(1)} fusion(bf16[8,32,1024]{2,1,0:T(8,128)(2,1)S(1)} %bitcast.53, bf16[3584,1024]{1,0:T(8,128)(2,1)} %param.13), kind=kOutput, calls=%fused_computation.10 | convolution fusion | flops 1879048192 | bytes 11534336 | tf_op jit(solution)/shard_map/jd,bsd->jsb/dot_general | solution.py:18
  247.1 2.1 fusion.7
  249.2 4.0 %copy.15 = f32[3584,32,8]{0,2,1:T(8,128)} copy(f32[3584,32,8]{0,1,2:T(8,128)S(1)} %fusion.7) | data formatting | bytes 7340032 | tf_op jit(solution)/shard_map/add | solution.py:19
  253.3 20.6 %gather_fusion.3 = bf16[3584,1024]{1,0:T(8,128)(2,1)} fusion(bf16[3584,1024]{1,0:T(8,128)(2,1)} %bitcast.12, s32[4096]{0:T(1024)S(1)} %pad_clamp_fusion), kind=kCustom, calls=%fused_computation.clone | custom fusion | bytes 14694400 | tf_op jit(solution)/shard_map/jit(_take)/gather | solution.py:41
  273.9 20.4 %gather_fusion.4 = bf16[3584,1024]{1,0:T(8,128)(2,1)} fusion(bf16[3584,1024]{1,0:T(8,128)(2,1)} %bitcast.14, s32[4096]{0:T(1024)S(1)} %pad_clamp_fusion), kind=kCustom, calls=%fused_computation.1.clone | custom fusion | bytes 14694400 | tf_op jit(solution)/shard_map/jit(_take)/gather | solution.py:41
  294.3 27.2 %all-to-all-done.3 = bf16[8,448,1024]{2,1,0:T(8,128)(2,1)} async-done(((bf16[8,448,1024]{2,1,0:T(8,128)(2,1)}), bf16[8,448,1024]{2,1,0:T(8,128)(2,1)}, u32[]{:S(2)}, u32[]{:S(2)}) %all-to-all-start.3) | async-done | bytes 7340064 | tf_op jit(solution)/shard_map/all_to_all | solution.py:36
  321.6 20.5 %gather_fusion.5 = bf16[3584,1024]{1,0:T(8,128)(2,1)} fusion(bf16[3584,1024]{1,0:T(8,128)(2,1)} %bitcast.16, s32[4096]{0:T(1024)S(1)} %pad_clamp_fusion), kind=kCustom, calls=%fused_computation.2.clone | custom fusion | bytes 14694400 | tf_op jit(solution)/shard_map/jit(_take)/gather | solution.py:41
  342.1 25.2 %multiply_convert_fusion = (bf16[3584,1024]{1,0:T(8,128)(2,1)}, bf16[3584,1024]{1,0:T(8,128)(2,1)}, bf16[3584,1024]{1,0:T(8,128)(2,1)}) fusion(bf16[3584,1024]{1,0:T(8,128)(2,1)} %param.11, bf16[3584,1024]{1,0:T(8,128)(2,1)} %gather_fusion.5, pred[3584]{0:T(1024)(128)(4,1)S(1)} %get-tuple-element.5, bf16[3584,1024]{1,0:T(8,128)(2,1)} %gather_fusion.4, ...), kind=kLoop, calls=%fused_computation.7 | loop fusion | flops 66060288 | bytes 66063872 | tf_op jit(solution)/shard_map/convert_element_type | solution.py:43
  367.3 2.2 broadcast_multiply_fusion
  (23 shorter events, 0.3 us)
Async XLA Ops:
  54.5 87.6 %all-to-all-start.1 = ((bf16[8,448,1024]{2,1,0:T(8,128)(2,1)}), bf16[8,448,1024]{2,1,0:T(8,128)(2,1)}, u32[]{:S(2)}, u32[]{:S(2)}) async-start(bf16[8,448,1024]{2,1,0:T(8,128)(2,1)} %bitcast.50), calls=%async_computation.2 | async-start | bytes 14680064 | tf_op jit(solution)/shard_map/all_to_all | solution.py:34
  142.1 91.9 %all-to-all-start.2 = ((bf16[8,448,1024]{2,1,0:T(8,128)(2,1)}), bf16[8,448,1024]{2,1,0:T(8,128)(2,1)}, u32[]{:S(2)}, u32[]{:S(2)}) async-start(bf16[8,448,1024]{2,1,0:T(8,128)(2,1)} %bitcast.49), calls=%async_computation.3 | async-start | bytes 14680064 | tf_op jit(solution)/shard_map/all_to_all | solution.py:35
  148.4 91.9 %all-gather.3.cloned.1.call-start = ((), (), s32[]{:S(2)}) async-start(), calls=%async_computation.6 | async-start | bytes 1179648 | tf_op jit(solution)/shard_map/all_gather | solution.py:16
  233.9 87.7 %all-to-all-start.3 = ((bf16[8,448,1024]{2,1,0:T(8,128)(2,1)}), bf16[8,448,1024]{2,1,0:T(8,128)(2,1)}, u32[]{:S(2)}, u32[]{:S(2)}) async-start(bf16[8,448,1024]{2,1,0:T(8,128)(2,1)} %bitcast.48), calls=%async_computation.4 | async-start | bytes 14680064 | tf_op jit(solution)/shard_map/all_to_all | solution.py:36
  240.2 6.9 %slice-start = ((s8[7340032]{0:T(1024)(128)(4,1)}), s8[3145728]{0:T(1024)(128)(4,1)S(1)}, s32[]{:S(2)}) async-start(s8[7340032]{0:T(1024)(128)(4,1)} %bitcast.46), calls=%async_computation.7 | async-start | bytes 6291456
  240.2 127.1 %reduce-scatter.2.cloned.1.call-start = ((), (), s32[]{:S(2)}) async-start(), calls=%async_computation.5 | async-start | bytes 4587520 | tf_op jit(solution)/shard_map/reduce_scatter | solution.py:22
  241.7 5.4 %slice-start.1 = ((s8[7340032]{0:T(1024)(128)(4,1)}), s8[4194304]{0:T(1024)(128)(4,1)S(1)}, s32[]{:S(2)}) async-start(s8[7340032]{0:T(1024)(128)(4,1)} %bitcast.46), calls=%async_computation.8 | async-start | bytes 8388608
  249.2 4.0 %copy-start = (s32[3584]{0:T(1024)S(1)}, s32[3584]{0:T(1024)}, u32[]{:S(2)}) copy-start(s32[3584]{0:T(1024)} %param.15) | copy-start | bytes 43012
Sparse Core Ops, SparseCore 0:
  155.6 33.0 all-gather.2
  253.4 69.0 reduce-scatter.1
where the time goes:
time: 379 us; the launch traced here: 376 us
  local copies, waits for them, and re-layouts  149 us (39%)
  waiting for transfers between devices  146 us (39%)
  other arithmetic  33.2 us (9%)
  starting transfers between devices  18.9 us (5%)
  between operations  14.2 us (4%)
  blocking collectives  7.58 us (2%)
  matrix products  7.48 us (2%)
    gather x3, local copies, waits for them, and re-layouts, local(): picked = jnp.take(flat_rows, slot_index, axis=0)  61.5 us
    all_to_all x1, waiting for transfers between devices, local(): lax.all_to_all(up_b[asked_rows], 'rows', split_axis=0, concat_axis=0, til...  60.9 us
    all_to_all x1, waiting for transfers between devices, local(): lax.all_to_all(gate_b[asked_rows], 'rows', split_axis=0, concat_axis=0, t...  58.1 us
    all_to_all x1, waiting for transfers between devices, local(): lax.all_to_all(down_b[asked_rows], 'rows', split_axis=0, concat_axis=0, t...  27.2 us
    convert_element_type x1, other arithmetic, local(): ((initial.astype(jnp.float32) + picked.astype(jnp.float32)) * 0.5).astype...  25.2 us
    gather x1, local copies, waits for them, and re-layouts, local(): up_b[asked_rows]  20.4 us
    gather x1, local copies, waits for them, and re-layouts, local(): down_b[asked_rows]  20.4 us
    gather x1, local copies, waits for them, and re-layouts, local(): gate_b[asked_rows]  20.4 us
  transfers between devices with their start and end apart: 5, of which 3 were waited for; matrix products, arithmetic and copies ran while one was open for 39% of the time, Pallas kernels for 0%

commit v1 on v0

v1 whole, which is shorter than its diff:
```python
import jax
import jax.numpy as jnp
from jax import lax
from jax.sharding import PartitionSpec as P

D = 4096
A_DEV = 32


def rows_gather(window):
    peers = lax.axis_size("rows")
    me = lax.axis_index("rows")
    held = window
    reach = 1
    while reach < peers:
        other = lax.ppermute(held, "rows", [(r, r ^ reach) for r in range(peers)])
        upper = (me // reach) % 2 == 1
        held = jnp.concatenate(
            [jnp.where(upper, other, held), jnp.where(upper, held, other)], axis=1
        )
        reach *= 2
    return held


def cols_reduce(parts):
    count = lax.axis_size("cols")
    me = lax.axis_index("cols")
    total = lax.dynamic_index_in_dim(parts, me, 0, keepdims=False)
    for shift in range(1, count):
        piece = lax.dynamic_index_in_dim(parts, (me + shift) % count, 0, keepdims=False)
        total = total + lax.ppermute(piece, "cols", [(c, (c + shift) % count) for c in range(count)])
    return total


def pick(array, index):
    return array.at[index].get(mode="promise_in_bounds")


def mix(initial, picked):
    return ((initial.astype(jnp.float32) + picked.astype(jnp.float32)) * 0.5).astype(jnp.bfloat16)


def local(up_a, gate_a, down_a, up_b, gate_b, down_b, perm):
    row_count = up_a.shape[0]
    features = up_a.shape[1]
    stride = row_count // A_DEV
    cost_scale = (2.0 * D) ** (-0.5)
    peers = lax.axis_size("rows")
    cols = lax.axis_size("cols")
    capacity = max(2, (row_count + peers - 1) // peers)

    source = perm // row_count
    local_row = perm % row_count
    blocks = jnp.arange(peers, dtype=jnp.int32)
    matches = (source[None, :] == blocks[:, None]).astype(jnp.int32)
    arrival_rank = jnp.sum(jnp.cumsum(matches, axis=1) * matches, axis=0) - 1
    high = (local_row // 256).astype(jnp.bfloat16)
    low = (local_row % 256).astype(jnp.bfloat16)
    halves = jnp.stack([high, low])[:, None, :] * matches.astype(jnp.bfloat16)[None]
    at_rank = (arrival_rank[None, :] == jnp.arange(capacity, dtype=jnp.int32)[:, None]).astype(jnp.bfloat16)
    found = jnp.einsum("hsi,ri->hsr", halves, at_rank, preferred_element_type=jnp.float32)
    wanted = found[0].astype(jnp.int32) * 256 + found[1].astype(jnp.int32)
    asked_rows = lax.all_to_all(wanted, "rows", split_axis=0, concat_axis=0, tiled=True)

    def exchange(array, index):
        return lax.all_to_all(pick(array, index), "rows", split_axis=0, concat_axis=0, tiled=True)

    window = jnp.stack([up_a[::stride], gate_a[::stride]])
    pieces = rows_gather(window[:, None])
    wide = pieces.transpose(0, 2, 1, 3).reshape(2, A_DEV * peers, features)
    partial_value = jnp.einsum("kd,jd->kj", wide[0], up_b, preferred_element_type=jnp.float32)
    partial_value = partial_value + jnp.einsum(
        "kd,jd->kj", wide[1], gate_b, preferred_element_type=jnp.float32
    )
    total = cols_reduce(partial_value.reshape(cols, -1, row_count))
    costs_out = (total * cost_scale).T

    first = capacity // 4 // 16 * 16
    if first > 0:
        early = exchange(up_b, asked_rows[:, :first])
        late = exchange(up_b, asked_rows[:, first:])
        held = jnp.concatenate(
            [early.reshape(peers * first, features), late.reshape(-1, features)], axis=0
        )
        slot_split = jnp.where(
            arrival_rank < first,
            source * first + arrival_rank,
            peers * first + source * (capacity - first) + arrival_rank - first,
        )
    else:
        held = exchange(up_b, asked_rows).reshape(-1, features)
        slot_split = source * capacity + arrival_rank
    slot = source * capacity + arrival_rank
    up_mean = mix(up_a, pick(held, slot_split))
    gate_moved = exchange(gate_b, asked_rows)
    gate_moved, up_mean = lax.optimization_barrier((gate_moved, up_mean))
    gate_mean = mix(gate_a, pick(gate_moved.reshape(-1, features), slot))

    cut = features * 3 // 4 // 128 * 128
    left = exchange(down_b[:, :cut], asked_rows)
    left, gate_mean = lax.optimization_barrier((left, gate_mean))
    left_mean = mix(down_a[:, :cut], pick(left.reshape(-1, cut), slot))
    down_mean = lax.dynamic_update_slice(jnp.zeros_like(down_a), left_mean, (0, 0))
    right = exchange(down_b[:, cut:], asked_rows)
    right, down_mean = lax.optimization_barrier((right, down_mean))
    right_mean = mix(down_a[:, cut:], pick(right.reshape(-1, features - cut), slot))
    down_mean = lax.dynamic_update_slice(down_mean, right_mean, (0, cut))
    return (costs_out, up_mean, gate_mean, down_mean)


def solution(mesh):
    placed = (P("rows", "cols"),) * 6 + (P("rows"),)
    return jax.shard_map(
        local,
        mesh=mesh,
        in_specs=placed,
        out_specs=(P("rows", "cols"),) * 4,
        check_vma=False,
    )
```

time: 379 us -> 471 us (1.24); the launches traced: 376 us -> 463 us
  waiting for transfers between devices: 146 us -> 192 us
  starting transfers between devices: 18.9 us -> 34.9 us
  other arithmetic: 33.2 us -> 48.6 us
  local copies, waits for them, and re-layouts: 149 us -> 164 us
  between operations: 14.2 us -> 1.31 us
  matrix products: 7.48 us -> 14.7 us
    ppermute x0 -> x6, waiting for transfers between devices: none -> 146 us  [the longest x3 78.5 us: rows_gather(): other = lax.ppermute(held, 'rows', [(r, r ^ reach) for r in range(peers)])]
    all_to_all x3 -> x5, waiting for transfers between devices: 146 us -> 46.1 us  [exchange(): lax.all_to_all(pick(array, index), 'rows', split_axis=0, concat_axis=0, t...]
    gather x6 -> x9, local copies, waits for them, and re-layouts: 123 us -> 144 us  [pick(): return array.at[index].get(mode='promise_in_bounds')]
    unnamed x7 -> x5, local copies, waits for them, and re-layouts: 13.7 us -> 1.86 us
    all_to_all x3 -> x5, starting transfers between devices: 18.9 us -> 29.2 us  [exchange(): lax.all_to_all(pick(array, index), 'rows', split_axis=0, concat_axis=0, t...]
    dot_general x2 -> x3, matrix products: 7.48 us -> 14.7 us  [the longest x1 7.19 us: local(): jnp.einsum('kd,jd->kj', wide[0], up_b, preferred_element_type=jnp.float32)]
    concatenate x0 -> x3, other arithmetic: none -> 7.1 us  [the longest x1 7.02 us: local(): jnp.concatenate([early.reshape(peers * first, features), late.reshape(-1,...]
    ppermute x0 -> x6, starting transfers between devices: none -> 5.68 us  [the longest x3 3.96 us: cols_reduce(): lax.ppermute(piece, 'cols', [(c, (c + shift) % count) for c in range(coun...]
  transfers between devices with their start and end apart: 5 -> 11, of which waited for: 3 -> 7; matrix products, arithmetic and copies ran while one was open for 39% -> 42% of each run, Pallas kernels for 0% -> 0%
where the time goes in v1:
time: 471 us; the launch traced here: 463 us
  waiting for transfers between devices  192 us (41%)
  local copies, waits for them, and re-layouts  164 us (35%)
  other arithmetic  48.6 us (10%)
  starting transfers between devices  34.9 us (7%)
  matrix products  14.7 us (3%)
  blocking collectives  7.58 us (2%)
    gather x9, local copies, waits for them, and re-layouts, pick(): return array.at[index].get(mode='promise_in_bounds')  144 us
    ppermute x3, waiting for transfers between devices, rows_gather(): other = lax.ppermute(held, 'rows', [(r, r ^ reach) for r in range(peers)])  78.5 us
    ppermute x3, waiting for transfers between devices, cols_reduce(): lax.ppermute(piece, 'cols', [(c, (c + shift) % count) for c in range(coun...  67.5 us
    all_to_all x5, waiting for transfers between devices, exchange(): lax.all_to_all(pick(array, index), 'rows', split_axis=0, concat_axis=0, t...  46.1 us
    convert_element_type x3, other arithmetic, mix(): ((initial.astype(jnp.float32) + picked.astype(jnp.float32)) * 0.5).astype...  29.9 us
    all_to_all x5, starting transfers between devices, exchange(): lax.all_to_all(pick(array, index), 'rows', split_axis=0, concat_axis=0, t...  29.2 us
  transfers between devices with their start and end apart: 11, of which 7 were waited for; matrix products, arithmetic and copies ran while one was open for 42% of the time, Pallas kernels for 0%

profile of v1, /device:TPU:11, one launch (start us, length us, event | category | flops | bytes accessed | tf_op | source)
XLA Modules:
  0.0 463.1 jit_solution(12606312241531014305)
XLA Ops:
  6.4 7.6 %all_to_all.37 = s32[8,1,448]{2,1,0:T(1,128)S(1)} all-to-all(s32[8,1,448]{2,1,0:T(1,128)S(1)} %copy.15), channel_id=1, replica_groups=mesh['rows'=8,'cols'=4] {'rows'}, dimensions={0} | all-to-all | bytes 28672 | tf_op jit(solution)/shard_map/all_to_all | solution.py:63
  14.1 9.6 %gather_fusion.1 = bf16[896,1024]{1,0:T(8,128)(2,1)} fusion(bf16[3584,1024]{1,0:T(8,128)(2,1)} %param.10, s32[1024]{0:T(1024)S(1)} %pad_clamp_fusion.4), kind=kCustom, calls=%fused_computation.1 | custom fusion | bytes 3673600 | tf_op jit(solution)/shard_map/gather | solution.py:36
  23.6 5.0 %all-to-all-start.2 = ((bf16[8,112,1024]{2,1,0:T(8,128)(2,1)}), bf16[8,112,1024]{2,1,0:T(8,128)(2,1)S(1)}, u32[]{:S(2)}, u32[]{:S(2)}) async-start(bf16[8,112,1024]{2,1,0:T(8,128)(2,1)} %bitcast.18), calls=%async_computation.2 | async-start | bytes 3670016 | tf_op jit(solution)/shard_map/all_to_all | solution.py:66
  28.8 17.1 %gather_fusion.2 = bf16[2688,1024]{1,0:T(8,128)(2,1)} fusion(bf16[3584,1024]{1,0:T(8,128)(2,1)} %param.10, s32[3072]{0:T(1024)S(1)} %pad_clamp_fusion.3), kind=kCustom, calls=%fused_computation.2 | custom fusion | bytes 11020800 | tf_op jit(solution)/shard_map/gather | solution.py:36
  45.9 5.0 %all-to-all-done.2 = bf16[8,112,1024]{2,1,0:T(8,128)(2,1)S(1)} async-done(((bf16[8,112,1024]{2,1,0:T(8,128)(2,1)}), bf16[8,112,1024]{2,1,0:T(8,128)(2,1)S(1)}, u32[]{:S(2)}, u32[]{:S(2)}) %all-to-all-start.2) | async-done | bytes 1835040 | tf_op jit(solution)/shard_map/all_to_all | solution.py:66
  50.9 6.2 %all-to-all-start.3 = ((bf16[8,336,1024]{2,1,0:T(8,128)(2,1)}), bf16[8,336,1024]{2,1,0:T(8,128)(2,1)}, u32[]{:S(2)}, u32[]{:S(2)}) async-start(bf16[8,336,1024]{2,1,0:T(8,128)(2,1)} %bitcast.69), calls=%async_computation.3 | async-start | bytes 11010048 | tf_op jit(solution)/shard_map/all_to_all | solution.py:66
  57.2 20.4 %gather_fusion = bf16[3584,1024]{1,0:T(8,128)(2,1)} fusion(bf16[3584,1024]{1,0:T(8,128)(2,1)} %param.11, s32[4096]{0:T(1024)S(1)} %pad_clamp_fusion.2), kind=kCustom, calls=%fused_computation | custom fusion | bytes 14694400 | tf_op jit(solution)/shard_map/gather | solution.py:36
  77.6 41.1 %all-to-all-done.3 = bf16[8,336,1024]{2,1,0:T(8,128)(2,1)} async-done(((bf16[8,336,1024]{2,1,0:T(8,128)(2,1)}), bf16[8,336,1024]{2,1,0:T(8,128)(2,1)}, u32[]{:S(2)}, u32[]{:S(2)}) %all-to-all-start.3) | async-done | bytes 5505056 | tf_op jit(solution)/shard_map/all_to_all | solution.py:66
  118.8 6.5 %all-to-all-start.1 = ((bf16[8,448,1024]{2,1,0:T(8,128)(2,1)}), bf16[8,448,1024]{2,1,0:T(8,128)(2,1)}, u32[]{:S(2)}, u32[]{:S(2)}) async-start(bf16[8,448,1024]{2,1,0:T(8,128)(2,1)} %bitcast.67), calls=%async_computation.1 | async-start | bytes 14680064 | tf_op jit(solution)/shard_map/all_to_all | solution.py:66
  125.3 3.2 slice.44
  128.5 3.2 slice.45
  133.4 77.6 %collective-permute-done.1 = bf16[2,2,32,1024]{3,2,0,1:T(8,128)(2,1)S(1)} collective-permute-done((bf16[2,2,32,1024]{3,2,0,1:T(8,128)(2,1)S(1)}, bf16[2,2,32,1024]{3,2,0,1:T(8,128)(2,1)S(1)}, u32[]{:S(2)}, u32[]{:S(2)}) %collective-permute-start.1) | collective-permute-done | bytes 262176 | tf_op jit(solution)/shard_map/ppermute | solution.py:16
  212.1 5.4 %slice.54 = bf16[3584,768]{1,0:T(8,128)(2,1)} slice(bf16[3584,1024]{1,0:T(8,128)(2,1)} %param.12), slice={[0:3584], [0:768]} | slice | bytes 11010048 | tf_op jit(solution)/shard_map/slice | solution.py:100
  217.5 17.2 %gather_fusion.4 = bf16[3584,768]{1,0:T(8,128)(2,1)} fusion(bf16[3584,768]{1,0:T(8,128)(2,1)} %slice.54, s32[4096]{0:T(1024)S(1)} %pad_clamp_fusion.2), kind=kCustom, calls=%fused_computation.4 | custom fusion | bytes 11024384 | tf_op jit(solution)/shard_map/gather | solution.py:36
  235.0 7.2 %fusion.10 = f32[256,3584]{1,0:T(8,128)} fusion(bf16[3584,1024]{1,0:T(8,128)(2,1)} %param.10, bf16[1,32,8,1024]{3,1,0,2:T(8,128)(2,1)S(1)} %get-tuple-element.20), kind=kOutput, calls=%fused_computation.31 | convolution fusion | flops 1879048192 | bytes 11534336 | tf_op jit(solution)/shard_map/kd,jd->kj/dot_general | solution.py:71
  242.1 6.9 %all-to-all-start.4 = ((bf16[8,448,768]{2,1,0:T(8,128)(2,1)}), bf16[8,448,768]{2,1,0:T(8,128)(2,1)}, u32[]{:S(2)}, u32[]{:S(2)}) async-start(bf16[8,448,768]{2,1,0:T(8,128)(2,1)} %bitcast.68), calls=%async_computation.4 | async-start | bytes 11010048 | tf_op jit(solution)/shard_map/all_to_all | solution.py:66
  249.0 6.3 %convolution_add_fusion = f32[256,3584]{1,0:T(8,128)S(1)} fusion(f32[256,3584]{1,0:T(8,128)} %fusion.10, bf16[3584,1024]{1,0:T(8,128)(2,1)} %param.11, bf16[1,32,8,1024]{3,1,0,2:T(8,128)(2,1)S(1)} %get-tuple-element.19), kind=kOutput, calls=%fused_computation.16 | convolution fusion | flops 1879965696 | bytes 15204352 | tf_op jit(solution)/shard_map/kd,jd->kj/dot_general | solution.py:72
  262.7 10.9 %gather_fusion.6 = bf16[3584,256]{1,0:T(8,128)(2,1)} fusion(bf16[3584,256]{1,0:T(8,128)(2,1)S(1)} %slice-done, s32[4096]{0:T(1024)S(1)} %pad_clamp_fusion.2), kind=kCustom, calls=%fused_computation.6 | custom fusion | bytes 3684352 | tf_op jit(solution)/shard_map/gather | solution.py:36
  273.6 6.9 %collective-permute-done.3 = f32[64,3584]{1,0:T(8,128)} collective-permute-done((f32[64,3584]{1,0:T(8,128)}, f32[64,3584]{1,0:T(8,128)}, u32[]{:S(2)}, u32[]{:S(2)}) %collective-permute-start.3) | collective-permute-done | bytes 917536 | tf_op jit(solution)/shard_map/ppermute | solution.py:31
  280.5 58.1 %collective-permute-done.4 = f32[64,3584]{1,0:T(8,128)} collective-permute-done((f32[64,3584]{1,0:T(8,128)}, f32[64,3584]{1,0:T(8,128)}, u32[]{:S(2)}, u32[]{:S(2)}) %collective-permute-start.4) | collective-permute-done | bytes 917536 | tf_op jit(solution)/shard_map/ppermute | solution.py:31
  341.1 3.1 fusion.8
  344.3 7.0 %pad_maximum_fusion = bf16[3584,1024]{1,0:T(8,128)(2,1)} fusion(bf16[2688,1024]{1,0:T(8,128)(2,1)} %bitcast.21, bf16[896,1024]{1,0:T(8,128)(2,1)} %bitcast.73), kind=kLoop, calls=%fused_computation.12 | loop fusion | flops 14680064 | bytes 14680064 | tf_op jit(solution)/shard_map/concatenate | solution.py:82
  351.3 20.4 %gather_fusion.3 = bf16[3584,1024]{1,0:T(8,128)(2,1)} fusion(bf16[3584,1024]{1,0:T(8,128)(2,1)} %pad_maximum_fusion, s32[4096]{0:T(1024)S(1)} %pad_clamp_fusion.1), kind=kCustom, calls=%fused_computation.3 | custom fusion | bytes 14694400 | tf_op jit(solution)/shard_map/gather | solution.py:36
  371.7 12.0 %multiply_convert_fusion.1 = bf16[3584,1024]{1,0:T(8,128)(2,1)} fusion(bf16[3584,1024]{1,0:T(8,128)(2,1)} %gather_fusion.3, bf16[3584,1024]{1,0:T(8,128)(2,1)} %param.7), kind=kLoop, calls=%fused_computation.10 | loop fusion | flops 18350080 | bytes 22020096 | tf_op jit(solution)/shard_map/convert_element_type | solution.py:40
  383.7 20.4 %gather_fusion.5 = bf16[3584,1024]{1,0:T(8,128)(2,1)} fusion(bf16[3584,1024]{1,0:T(8,128)(2,1)} %bitcast.23, s32[4096]{0:T(1024)S(1)} %pad_clamp_fusion), kind=kCustom, calls=%fused_computation.5 | custom fusion | bytes 14694400 | tf_op jit(solution)/shard_map/gather | solution.py:36
  404.1 4.6 all-to-all-start.5
  408.8 12.0 %multiply_convert_fusion = bf16[3584,1024]{1,0:T(8,128)(2,1)} fusion(bf16[3584,1024]{1,0:T(8,128)(2,1)} %gather_fusion.5, bf16[3584,1024]{1,0:T(8,128)(2,1)} %param.8), kind=kLoop, calls=%fused_computation.9 | loop fusion | flops 18350080 | bytes 22020096 | tf_op jit(solution)/shard_map/convert_element_type | solution.py:40
  420.8 17.2 %gather_fusion.7 = bf16[3584,768]{1,0:T(8,128)(2,1)} fusion(bf16[3584,768]{1,0:T(8,128)(2,1)} %bitcast.25, s32[4096]{0:T(1024)S(1)} %pad_clamp_fusion), kind=kCustom, calls=%fused_computation.7 | custom fusion | bytes 11024384 | tf_op jit(solution)/shard_map/gather | solution.py:36
  438.0 5.9 %multiply_convert_fusion.2 = bf16[3584,768]{1,0:T(8,128)(2,1)S(1)} fusion(bf16[3584,768]{1,0:T(8,128)(2,1)} %gather_fusion.7, bf16[3584,1024]{1,0:T(8,128)(2,1)} %param.9), kind=kLoop, calls=%fused_computation.11 | loop fusion | flops 13762560 | bytes 16515072 | tf_op jit(solution)/shard_map/convert_element_type | solution.py:40
  443.8 4.1 dynamic_update_slice.6
  447.9 10.9 %gather_fusion.8 = bf16[3584,256]{1,0:T(8,128)(2,1)} fusion(bf16[3584,256]{1,0:T(8,128)(2,1)S(1)} %bitcast.66, s32[4096]{0:T(1024)S(1)} %pad_clamp_fusion), kind=kCustom, calls=%fused_computation.8 | custom fusion | bytes 3684352 | tf_op jit(solution)/shard_map/gather | solution.py:36
  458.8 3.8 fusion.4
  (54 shorter events, 19.0 us)
Async XLA Ops:
  23.6 27.3 %all-to-all-start.2 = ((bf16[8,112,1024]{2,1,0:T(8,128)(2,1)}), bf16[8,112,1024]{2,1,0:T(8,128)(2,1)S(1)}, u32[]{:S(2)}, u32[]{:S(2)}) async-start(bf16[8,112,1024]{2,1,0:T(8,128)(2,1)} %bitcast.18), calls=%async_computation.2 | async-start | bytes 3670016 | tf_op jit(solution)/shard_map/all_to_all | solution.py:66
  50.9 26.7 %copy-start.1 = (bf16[8,112,1024]{2,1,0:T(8,128)(2,1)}, bf16[8,112,1024]{2,1,0:T(8,128)(2,1)S(1)}, u32[]{:S(2)}) copy-start(bf16[8,112,1024]{2,1,0:T(8,128)(2,1)S(1)} %all-to-all-done.2) | copy-start | bytes 5505028
  50.9 67.8 %all-to-all-start.3 = ((bf16[8,336,1024]{2,1,0:T(8,128)(2,1)}), bf16[8,336,1024]{2,1,0:T(8,128)(2,1)}, u32[]{:S(2)}, u32[]{:S(2)}) async-start(bf16[8,336,1024]{2,1,0:T(8,128)(2,1)} %bitcast.69), calls=%async_computation.3 | async-start | bytes 11010048 | tf_op jit(solution)/shard_map/all_to_all | solution.py:66
  118.8 123.4 %all-to-all-start.1 = ((bf16[8,448,1024]{2,1,0:T(8,128)(2,1)}), bf16[8,448,1024]{2,1,0:T(8,128)(2,1)}, u32[]{:S(2)}, u32[]{:S(2)}) async-start(bf16[8,448,1024]{2,1,0:T(8,128)(2,1)} %bitcast.67), calls=%async_computation.1 | async-start | bytes 14680064 | tf_op jit(solution)/shard_map/all_to_all | solution.py:66
  131.7 1.4 collective-permute-start
  133.2 77.7 %collective-permute-start.1 = (bf16[2,2,32,1024]{3,2,0,1:T(8,128)(2,1)S(1)}, bf16[2,2,32,1024]{3,2,0,1:T(8,128)(2,1)S(1)}, u32[]{:S(2)}, u32[]{:S(2)}) collective-permute-start(bf16[2,2,32,1024]{3,2,0,1:T(8,128)(2,1)S(1)} %pad_maximum_fusion.2), channel_id=1, source_target_pairs={{0,8},{4,12},{8,0},{12,4},{16,24},{20,28},{24,16},{28,20},{1,9},{5... | collective-permute-start | bytes 786440 | tf_op jit(solution)/shard_map/ppermute | solution.py:16
  211.0 23.7 %collective-permute-start.2 = (bf16[2,4,32,1024]{3,2,0,1:T(8,128)(2,1)S(1)}, bf16[2,4,32,1024]{3,2,0,1:T(8,128)(2,1)S(1)}, u32[]{:S(2)}, u32[]{:S(2)}) collective-permute-start(bf16[2,4,32,1024]{3,2,0,1:T(8,128)(2,1)S(1)} %pad_maximum_fusion.1), channel_id=1, source_target_pairs={{0,16},{4,20},{8,24},{12,28},{16,0},{20,4},{24,8},{28,12},{1,17},{... | collective-permute-start | bytes 1572872 | tf_op jit(solution)/shard_map/ppermute | solution.py:16
  242.1 162.0 %all-to-all-start.4 = ((bf16[8,448,768]{2,1,0:T(8,128)(2,1)}), bf16[8,448,768]{2,1,0:T(8,128)(2,1)}, u32[]{:S(2)}, u32[]{:S(2)}) async-start(bf16[8,448,768]{2,1,0:T(8,128)(2,1)} %bitcast.68), calls=%async_computation.4 | async-start | bytes 11010048 | tf_op jit(solution)/shard_map/all_to_all | solution.py:66
  255.4 1.9 copy-start
  255.4 7.3 %slice-start = ((bf16[3584,1024]{1,0:T(8,128)(2,1)}), bf16[3584,256]{1,0:T(8,128)(2,1)S(1)}, s32[]{:S(2)}) async-start(bf16[3584,1024]{1,0:T(8,128)(2,1)} %param.12), calls=%async_computation.6 | async-start | bytes 3670016 | tf_op jit(solution)/shard_map/slice | solution.py:104
  258.7 21.8 %collective-permute-start.3 = (f32[64,3584]{1,0:T(8,128)}, f32[64,3584]{1,0:T(8,128)}, u32[]{:S(2)}, u32[]{:S(2)}) collective-permute-start(f32[64,3584]{1,0:T(8,128)} %get-tuple-element.16), channel_id=1, source_target_pairs={{0,1},{1,2},{2,3},{3,0},{4,5},{5,6},{6,7},{7,4},{8,9},{9,10},{10,1... | collective-permute-start | bytes 2752520 | tf_op jit(solution)/shard_map/ppermute | solution.py:31
  260.0 78.6 %collective-permute-start.4 = (f32[64,3584]{1,0:T(8,128)}, f32[64,3584]{1,0:T(8,128)}, u32[]{:S(2)}, u32[]{:S(2)}) collective-permute-start(f32[64,3584]{1,0:T(8,128)} %get-tuple-element.18), channel_id=1, source_target_pairs={{0,2},{1,3},{2,0},{3,1},{4,6},{5,7},{6,4},{7,5},{8,10},{9,11},{10,... | collective-permute-start | bytes 2752520 | tf_op jit(solution)/shard_map/ppermute | solution.py:31
  261.0 80.1 %collective-permute-start.5 = (f32[64,3584]{1,0:T(8,128)S(1)}, f32[64,3584]{1,0:T(8,128)}, u32[]{:S(2)}, u32[]{:S(2)}) collective-permute-start(f32[64,3584]{1,0:T(8,128)S(1)} %get-tuple-element.17), channel_id=1, source_target_pairs={{0,3},{1,0},{2,1},{3,2},{4,7},{5,4},{6,5},{7,6},{8,11},{9,8},{10,9... | collective-permute-start | bytes 2752520 | tf_op jit(solution)/shard_map/ppermute | solution.py:31
  404.1 43.8 %all-to-all-start.5 = ((bf16[8,448,256]{2,1,0:T(8,128)(2,1)}), bf16[8,448,256]{2,1,0:T(8,128)(2,1)S(1)}, u32[]{:S(2)}, u32[]{:S(2)}) async-start(bf16[8,448,256]{2,1,0:T(8,128)(2,1)} %bitcast.72), calls=%async_computation.5 | async-start | bytes 3670016 | tf_op jit(solution)/shard_map/all_to_all | solution.py:66

commit v2 on v1

v2 whole, which is shorter than its diff:
```python
import jax
import jax.numpy as jnp
from jax import lax
from jax.sharding import PartitionSpec as P

D = 4096
A_DEV = 32


def rows_gather(window):
    peers = lax.axis_size("rows")
    me = lax.axis_index("rows")
    held = window[:, :, None]
    reach = peers // 2
    while reach >= 1:
        other = lax.ppermute(held, "rows", [(r, r ^ reach) for r in range(peers)])
        upper = (me // reach) % 2 == 1
        pair = jnp.stack([jnp.where(upper, other, held), jnp.where(upper, held, other)], axis=3)
        held = pair.reshape(pair.shape[0], pair.shape[1], -1, pair.shape[4])
        reach //= 2
    return held


def cols_reduce(parts):
    count = lax.axis_size("cols")
    me = lax.axis_index("cols")
    moved = [lax.dynamic_index_in_dim(parts, me, 0, keepdims=False)]
    for shift in range(1, count):
        piece = lax.dynamic_index_in_dim(parts, (me + shift) % count, 0, keepdims=False)
        moved.append(lax.ppermute(piece, "cols", [(c, (c + shift) % count) for c in range(count)]))
    return moved


def pick(array, index):
    return array.at[index].get(mode="promise_in_bounds")


def mix(initial, picked):
    return ((initial.astype(jnp.float32) + picked.astype(jnp.float32)) * 0.5).astype(jnp.bfloat16)


def local(up_a, gate_a, down_a, up_b, gate_b, down_b, perm):
    row_count = up_a.shape[0]
    features = up_a.shape[1]
    stride = row_count // A_DEV
    cost_scale = (2.0 * D) ** (-0.5)
    peers = lax.axis_size("rows")
    cols = lax.axis_size("cols")
    capacity = max(2, (row_count + peers - 1) // peers)

    source = perm // row_count
    local_row = perm % row_count
    blocks = jnp.arange(peers, dtype=jnp.int32)
    matches = (source[None, :] == blocks[:, None]).astype(jnp.int32)
    arrival_rank = jnp.sum(jnp.cumsum(matches, axis=1) * matches, axis=0) - 1
    high = (local_row // 256).astype(jnp.bfloat16)
    low = (local_row % 256).astype(jnp.bfloat16)
    halves = jnp.stack([high, low])[:, None, :] * matches.astype(jnp.bfloat16)[None]
    at_rank = (arrival_rank[None, :] == jnp.arange(capacity, dtype=jnp.int32)[:, None]).astype(jnp.bfloat16)
    found = jnp.einsum("hsi,ri->hsr", halves, at_rank, preferred_element_type=jnp.float32)
    wanted = found[0].astype(jnp.int32) * 256 + found[1].astype(jnp.int32)
    asked_rows = lax.all_to_all(wanted, "rows", split_axis=0, concat_axis=0, tiled=True)

    def exchange(rows):
        moved = rows.reshape(peers, -1, rows.shape[1])
        moved = lax.all_to_all(moved, "rows", split_axis=0, concat_axis=0, tiled=True)
        return moved.reshape(-1, rows.shape[1])

    asked = asked_rows.reshape(-1)
    slot = source * capacity + arrival_rank

    pieces = rows_gather(jnp.stack([up_a[::stride], gate_a[::stride]]))
    wide = pieces.reshape(2, A_DEV * peers, features)

    up_rows = pick(up_b, asked)
    up_rows, wide = lax.optimization_barrier((up_rows, wide))
    up_moved = exchange(up_rows)

    partial_value = jnp.einsum("kd,jd->kj", wide[0], up_b, preferred_element_type=jnp.float32)
    partial_value = partial_value + jnp.einsum(
        "kd,jd->kj", wide[1], gate_b, preferred_element_type=jnp.float32
    )
    gate_rows = pick(gate_b, asked)
    gate_rows, partial_value = lax.optimization_barrier((gate_rows, partial_value))
    terms = cols_reduce(partial_value.reshape(cols, -1, row_count))

    cut = features * 3 // 4 // 128 * 128
    left_rows = pick(down_b[:, :cut], asked)
    right_rows = pick(down_b[:, cut:], asked)

    gate_moved = exchange(gate_rows)
    up_mean = mix(up_a, pick(up_moved, slot))
    tied = lax.optimization_barrier((left_rows, right_rows, up_mean) + tuple(terms[1::2]))
    left_rows, right_rows, up_mean = tied[:3]
    terms[1::2] = tied[3:]
    left = exchange(left_rows)
    gate_mean = mix(gate_a, pick(gate_moved, slot))
    tied = lax.optimization_barrier((right_rows, gate_mean) + tuple(terms[::2]))
    right_rows, gate_mean = tied[:2]
    terms[::2] = tied[2:]
    right = exchange(right_rows)
    left_mean = mix(down_a[:, :cut], pick(left, slot))
    down_mean = lax.dynamic_update_slice(jnp.zeros_like(down_a), left_mean, (0, 0))
    total = terms[0]
    for term in terms[1:]:
        total = total + term
    costs_out = (total * cost_scale).T
    right, down_mean, costs_out = lax.optimization_barrier((right, down_mean, costs_out))
    right_mean = mix(down_a[:, cut:], pick(right, slot))
    down_mean = lax.dynamic_update_slice(down_mean, right_mean, (0, cut))
    return (costs_out, up_mean, gate_mean, down_mean)


def solution(mesh):
    placed = (P("rows", "cols"),) * 6 + (P("rows"),)
    return jax.shard_map(
        local,
        mesh=mesh,
        in_specs=placed,
        out_specs=(P("rows", "cols"),) * 4,
        check_vma=False,
    )
```

time: 471 us -> 347 us (0.74); the launches traced: 463 us -> 345 us
  waiting for transfers between devices: 192 us -> 97.1 us
  blocking collectives: 7.58 us -> 0 us
  other arithmetic: 48.6 us -> 41.2 us
    ppermute x3, waiting for transfers between devices: 78.5 us -> 6.58 us  [rows_gather(): other = lax.ppermute(held, 'rows', [(r, r ^ reach) for r in range(peers)])]
    ppermute x3, waiting for transfers between devices: 67.5 us -> 16.7 us  [cols_reduce(): lax.ppermute(piece, 'cols', [(c, (c + shift) % count) for c in range(coun...]
    all_to_all x5, waiting for transfers between devices: 46.1 us -> 73.8 us  [the longest x4 70.6 us: exchange(): lax.all_to_all(moved, 'rows', split_axis=0, concat_axis=0, tiled=True)]
    all_to_all x1 -> x0, blocking collectives: 7.58 us -> none  [local(): lax.all_to_all(wanted, 'rows', split_axis=0, concat_axis=0, tiled=True)]
    concatenate x3 -> x0, other arithmetic: 7.1 us -> none  [the longest x1 7.02 us: local(): jnp.concatenate([early.reshape(peers * first, features), late.reshape(-1,...]
    gather x9 -> x8, local copies, waits for them, and re-layouts: 144 us -> 138 us  [pick(): return array.at[index].get(mode='promise_in_bounds')]
  transfers between devices with their start and end apart: 11 -> 11, of which waited for: 7 -> 7; matrix products, arithmetic and copies ran while one was open for 42% -> 55% of each run, Pallas kernels for 0% -> 0%
where the time goes in v2:
time: 347 us; the launch traced here: 345 us
  local copies, waits for them, and re-layouts  161 us (46%)
  waiting for transfers between devices  97.1 us (28%)
  other arithmetic  41.2 us (12%)
  starting transfers between devices  34.5 us (10%)
  matrix products  10.4 us (3%)
    gather x8, local copies, waits for them, and re-layouts, pick(): return array.at[index].get(mode='promise_in_bounds')  138 us
    all_to_all x4, waiting for transfers between devices, exchange(): lax.all_to_all(moved, 'rows', split_axis=0, concat_axis=0, tiled=True)  70.6 us
    convert_element_type x3, other arithmetic, mix(): ((initial.astype(jnp.float32) + picked.astype(jnp.float32)) * 0.5).astype...  29.9 us
    all_to_all x4, starting transfers between devices, exchange(): lax.all_to_all(moved, 'rows', split_axis=0, concat_axis=0, tiled=True)  23.8 us
    ppermute x3, waiting for transfers between devices, cols_reduce(): lax.ppermute(piece, 'cols', [(c, (c + shift) % count) for c in range(coun...  16.7 us
  transfers between devices with their start and end apart: 11, of which 7 were waited for; matrix products, arithmetic and copies ran while one was open for 55% of the time, Pallas kernels for 0%

profile of v2, /device:TPU:11, one launch (start us, length us, event | category | flops | bytes accessed | tf_op | source)
XLA Modules:
  0.0 345.2 jit_solution(5310678359253872684)
XLA Ops:
  0.6 3.2 slice.42
  3.8 3.2 slice.43
  9.1 2.3 reduce-window.6
  13.4 6.6 %collective-permute-done.1 = bf16[2,32,2,1024]{3,1,2,0:T(8,128)(2,1)S(1)} collective-permute-done((bf16[2,32,2,1024]{3,1,2,0:T(8,128)(2,1)S(1)}, bf16[2,32,2,1024]{3,1,2,0:T(8,128)(2,1)S(1)}, u32[]{:S(2)}, u32[]{:S(2)}) %collective-permute-start.1) | collective-permute-done | bytes 262176 | tf_op jit(solution)/shard_map/ppermute | solution.py:16
  23.7 3.4 all-to-all-start
  27.1 3.3 all-to-all-done
  30.6 20.4 %gather_fusion.2 = bf16[3584,1024]{1,0:T(8,128)(2,1)} fusion(bf16[3584,1024]{1,0:T(8,128)(2,1)} %param.10, s32[4096]{0:T(1024)S(1)} %pad_clamp_fusion.1), kind=kCustom, calls=%fused_computation.2 | custom fusion | bytes 14694400 | tf_op jit(solution)/shard_map/gather | solution.py:35
  52.3 6.3 %all-to-all-start.1 = ((bf16[8,448,1024]{2,1,0:T(8,128)(2,1)}), bf16[8,448,1024]{2,1,0:T(8,128)(2,1)}, u32[]{:S(2)}, u32[]{:S(2)}) async-start(bf16[8,448,1024]{2,1,0:T(8,128)(2,1)} %bitcast.75), calls=%async_computation.1 | async-start | bytes 14680064 | tf_op jit(solution)/shard_map/all_to_all | solution.py:66
  58.6 20.4 %gather_fusion.4 = bf16[3584,1024]{1,0:T(8,128)(2,1)} fusion(bf16[3584,1024]{1,0:T(8,128)(2,1)} %param.11, s32[4096]{0:T(1024)S(1)} %pad_clamp_fusion.1), kind=kCustom, calls=%fused_computation.4 | custom fusion | bytes 14694400 | tf_op jit(solution)/shard_map/gather | solution.py:35
  80.5 5.3 %fusion.7 = f32[256,3584]{1,0:T(8,128)S(1)} fusion(bf16[3584,1024]{1,0:T(8,128)(2,1)} %param.10, bf16[1,256,1024]{2,0,1:T(2,128)(2,1)S(1)} %get-tuple-element.41), kind=kOutput, calls=%fused_computation.27 | convolution fusion | flops 1879048192 | bytes 11534336 | tf_op jit(solution)/shard_map/kd,jd->kj/dot_general | solution.py:79
  85.8 3.9 %convolution_add_fusion = f32[256,3584]{1,0:T(8,128)} fusion(f32[256,3584]{1,0:T(8,128)S(1)} %fusion.7, bf16[3584,1024]{1,0:T(8,128)(2,1)S(1)} %bitcast.72, bf16[1,256,1024]{2,0,1:T(2,128)(2,1)S(1)} %get-tuple-element.40), kind=kOutput, calls=%fused_computation.14 | convolution fusion | flops 1879965696 | bytes 15204352 | tf_op jit(solution)/shard_map/kd,jd->kj/dot_general | solution.py:80
  89.8 50.1 %all-to-all-done.1 = bf16[8,448,1024]{2,1,0:T(8,128)(2,1)} async-done(((bf16[8,448,1024]{2,1,0:T(8,128)(2,1)}), bf16[8,448,1024]{2,1,0:T(8,128)(2,1)}, u32[]{:S(2)}, u32[]{:S(2)}) %all-to-all-start.1) | async-done | bytes 7340064 | tf_op jit(solution)/shard_map/all_to_all | solution.py:66
  139.9 6.3 %all-to-all-start.2 = ((bf16[8,448,1024]{2,1,0:T(8,128)(2,1)}), bf16[8,448,1024]{2,1,0:T(8,128)(2,1)}, u32[]{:S(2)}, u32[]{:S(2)}) async-start(bf16[8,448,1024]{2,1,0:T(8,128)(2,1)} %bitcast.74), calls=%async_computation.2 | async-start | bytes 14680064 | tf_op jit(solution)/shard_map/all_to_all | solution.py:66
  146.2 5.4 %slice.36 = bf16[3584,768]{1,0:T(8,128)(2,1)} slice(bf16[3584,1024]{1,0:T(8,128)(2,1)} %param.12), slice={[0:3584], [0:768]} | slice | bytes 11010048 | tf_op jit(solution)/shard_map/slice | solution.py:88
  151.6 17.3 %gather_fusion = bf16[3584,768]{1,0:T(8,128)(2,1)} fusion(bf16[3584,768]{1,0:T(8,128)(2,1)} %slice.36, s32[4096]{0:T(1024)S(1)} %pad_clamp_fusion.1), kind=kCustom, calls=%fused_computation | custom fusion | bytes 11024384 | tf_op jit(solution)/shard_map/gather | solution.py:35
  168.9 10.9 %gather_fusion.1 = bf16[3584,256]{1,0:T(8,128)(2,1)} fusion(bf16[3584,256]{1,0:T(8,128)(2,1)S(1)} %slice-done.2, s32[4096]{0:T(1024)S(1)} %pad_clamp_fusion.1), kind=kCustom, calls=%fused_computation.1 | custom fusion | bytes 3684352 | tf_op jit(solution)/shard_map/gather | solution.py:35
  179.8 3.6 %dynamic-slice_bitcast_fusion = (f32[64,3584]{1,0:T(8,128)}, f32[64,3584]{1,0:T(8,128)S(1)}, f32[64,3584]{1,0:T(8,128)}, f32[64,3584]{1,0:T(8,128)}) fusion(f32[4,64,3584]{2,1,0:T(8,128)} %bitcast.77, s32[]{:T(128)S(6)} %select_n.147, s32[]{:T(128)S(6)} %select_n.145, s32[]{:T(128)S(6)} %select_n.144, s32[]{:T(128)S(6)} %select_n.142), kind=kLoop, calls=%fused_computation.20 | loop fusion | bytes 7340048 | tf_op jit(solution)/shard_map/jit(dynamic_index_in_dim)/squeeze | solution.py:29
  184.9 20.4 %gather_fusion.3 = bf16[3584,1024]{1,0:T(8,128)(2,1)} fusion(bf16[3584,1024]{1,0:T(8,128)(2,1)} %bitcast.19, s32[4096]{0:T(1024)S(1)} %pad_clamp_fusion), kind=kCustom, calls=%fused_computation.3 | custom fusion | bytes 14694400 | tf_op jit(solution)/shard_map/gather | solution.py:35
  205.3 12.0 %multiply_convert_fusion.1 = bf16[3584,1024]{1,0:T(8,128)(2,1)} fusion(bf16[3584,1024]{1,0:T(8,128)(2,1)} %gather_fusion.3, bf16[3584,1024]{1,0:T(8,128)(2,1)} %param.7), kind=kLoop, calls=%fused_computation.9 | loop fusion | flops 18350080 | bytes 22020096 | tf_op jit(solution)/shard_map/convert_element_type | solution.py:39
  217.4 9.2 %collective-permute-done.4 = f32[64,3584]{1,0:T(8,128)S(1)} collective-permute-done((f32[64,3584]{1,0:T(8,128)}, f32[64,3584]{1,0:T(8,128)S(1)}, u32[]{:S(2)}, u32[]{:S(2)}) %collective-permute-start.4) | collective-permute-done | bytes 917536 | tf_op jit(solution)/shard_map/ppermute | solution.py:30
  227.6 6.1 %all-to-all-start.4 = ((bf16[8,448,768]{2,1,0:T(8,128)(2,1)}), bf16[8,448,768]{2,1,0:T(8,128)(2,1)}, u32[]{:S(2)}, u32[]{:S(2)}) async-start(bf16[8,448,768]{2,1,0:T(8,128)(2,1)} %bitcast.76), calls=%async_computation.4 | async-start | bytes 11010048 | tf_op jit(solution)/shard_map/all_to_all | solution.py:66
  236.0 20.4 %gather_fusion.5 = bf16[3584,1024]{1,0:T(8,128)(2,1)} fusion(bf16[3584,1024]{1,0:T(8,128)(2,1)} %bitcast.24, s32[4096]{0:T(1024)S(1)} %pad_clamp_fusion), kind=kCustom, calls=%fused_computation.5 | custom fusion | bytes 14694400 | tf_op jit(solution)/shard_map/gather | solution.py:35
  256.4 12.0 %multiply_convert_fusion = bf16[3584,1024]{1,0:T(8,128)(2,1)} fusion(bf16[3584,1024]{1,0:T(8,128)(2,1)} %gather_fusion.5, bf16[3584,1024]{1,0:T(8,128)(2,1)} %param.8), kind=kLoop, calls=%fused_computation.8 | loop fusion | flops 18350080 | bytes 22020096 | tf_op jit(solution)/shard_map/convert_element_type | solution.py:39
  268.5 7.5 %collective-permute-done.5 = f32[64,3584]{1,0:T(8,128)} collective-permute-done((f32[64,3584]{1,0:T(8,128)}, f32[64,3584]{1,0:T(8,128)}, u32[]{:S(2)}, u32[]{:S(2)}) %collective-permute-start.5) | collective-permute-done | bytes 917536 | tf_op jit(solution)/shard_map/ppermute | solution.py:30
  276.0 19.4 %all-to-all-done.4 = bf16[8,448,768]{2,1,0:T(8,128)(2,1)} async-done(((bf16[8,448,768]{2,1,0:T(8,128)(2,1)}), bf16[8,448,768]{2,1,0:T(8,128)(2,1)}, u32[]{:S(2)}, u32[]{:S(2)}) %all-to-all-start.4) | async-done | bytes 5505056 | tf_op jit(solution)/shard_map/all_to_all | solution.py:66
  295.4 5.1 %all-to-all-start.3 = ((bf16[8,448,256]{2,1,0:T(8,128)(2,1)}), bf16[8,448,256]{2,1,0:T(8,128)(2,1)S(1)}, u32[]{:S(2)}, u32[]{:S(2)}) async-start(bf16[8,448,256]{2,1,0:T(8,128)(2,1)} %bitcast.79), calls=%async_computation.3 | async-start | bytes 3670016 | tf_op jit(solution)/shard_map/all_to_all | solution.py:66
  300.5 2.8 multiply_bitcast_fusion
  303.3 17.2 %gather_fusion.6 = bf16[3584,768]{1,0:T(8,128)(2,1)} fusion(bf16[3584,768]{1,0:T(8,128)(2,1)} %bitcast.30, s32[4096]{0:T(1024)S(1)} %pad_clamp_fusion), kind=kCustom, calls=%fused_computation.6 | custom fusion | bytes 11024384 | tf_op jit(solution)/shard_map/gather | solution.py:35
  320.5 5.9 %multiply_convert_fusion.2 = bf16[3584,768]{1,0:T(8,128)(2,1)S(1)} fusion(bf16[3584,768]{1,0:T(8,128)(2,1)} %gather_fusion.6, bf16[3584,1024]{1,0:T(8,128)(2,1)} %param.9), kind=kLoop, calls=%fused_computation.10 | loop fusion | flops 13762560 | bytes 16515072 | tf_op jit(solution)/shard_map/convert_element_type | solution.py:39
  326.4 4.1 %dynamic_update_slice.6 = bf16[3584,1024]{1,0:T(8,128)(2,1)} pad(bf16[3584,768]{1,0:T(8,128)(2,1)S(1)} %multiply_convert_fusion.2, bf16[]{:T(256)} %constant.143.clone.1), padding=0_0x0_256 | pad | bytes 12845058 | tf_op jit(solution)/shard_map/dynamic_update_slice | solution.py:103
  330.4 10.9 %gather_fusion.7 = bf16[3584,256]{1,0:T(8,128)(2,1)} fusion(bf16[3584,256]{1,0:T(8,128)(2,1)S(1)} %bitcast.73, s32[4096]{0:T(1024)S(1)} %pad_clamp_fusion), kind=kCustom, calls=%fused_computation.7 | custom fusion | bytes 3684352 | tf_op jit(solution)/shard_map/gather | solution.py:35
  341.4 3.8 %fusion.4 = bf16[3584,1024]{1,0:T(8,128)(2,1)} fusion(bf16[3584,1024]{1,0:T(8,128)(2,1)} %dynamic_update_slice.6, bf16[3584,256]{1,0:T(8,128)(2,1)} %gather_fusion.7, bf16[3584,1024]{1,0:T(8,128)(2,1)} %param.9), kind=kLoop, calls=%fused_computation.17 | loop fusion | flops 4587520 | bytes 5505024 | tf_op jit(solution)/shard_map/dynamic_update_slice | solution.py:110
  (50 shorter events, 15.4 us)
Async XLA Ops:
  7.1 5.8 %collective-permute-start = (bf16[2,32,1,1024]{3,1,0,2:T(8,128)(2,1)S(1)}, bf16[2,32,1,1024]{3,1,0,2:T(8,128)(2,1)S(1)}, u32[]{:S(2)}, u32[]{:S(2)}) collective-permute-start(bf16[2,32,1,1024]{3,1,0,2:T(8,128)(2,1)S(1)} %maximum_bitcast_fusion.1), channel_id=1, source_target_pairs={{0,16},{4,20},{8,24},{12,28},{16,0},{20,4},{24,8},{28,12},{1,17},{... | collective-permute-start | bytes 393224 | tf_op jit(solution)/shard_map/ppermute | solution.py:16
  13.0 7.0 %collective-permute-start.1 = (bf16[2,32,2,1024]{3,1,2,0:T(8,128)(2,1)S(1)}, bf16[2,32,2,1024]{3,1,2,0:T(8,128)(2,1)S(1)}, u32[]{:S(2)}, u32[]{:S(2)}) collective-permute-start(bf16[2,32,2,1024]{3,1,2,0:T(8,128)(2,1)S(1)} %maximum_bitcast_fusion), channel_id=1, source_target_pairs={{0,8},{4,12},{8,0},{12,4},{16,24},{20,28},{24,16},{28,20},{1,9},{5... | collective-permute-start | bytes 786440 | tf_op jit(solution)/shard_map/ppermute | solution.py:16
  20.1 30.9 %collective-permute-start.2 = (bf16[2,32,4,1024]{3,1,2,0:T(8,128)(2,1)S(1)}, bf16[2,32,4,1024]{3,1,2,0:T(8,128)(2,1)S(1)}, u32[]{:S(2)}, u32[]{:S(2)}) collective-permute-start(bf16[2,32,4,1024]{3,1,2,0:T(8,128)(2,1)S(1)} %bitcast.80), channel_id=1, source_target_pairs={{0,4},{4,0},{8,12},{12,8},{16,20},{20,16},{24,28},{28,24},{1,5},{5... | collective-permute-start | bytes 1572872 | tf_op jit(solution)/shard_map/ppermute | solution.py:16
  23.7 6.7 %all-to-all-start = ((s32[8,1,448]{2,1,0:T(1,128)}), s32[8,1,448]{2,1,0:T(1,128)S(1)}, u32[]{:S(2)}, u32[]{:S(2)}) async-start(s32[8,1,448]{2,1,0:T(1,128)} %copy.17), calls=%async_computation | async-start | bytes 32768 | tf_op jit(solution)/shard_map/all_to_all | solution.py:62
  52.3 87.6 %all-to-all-start.1 = ((bf16[8,448,1024]{2,1,0:T(8,128)(2,1)}), bf16[8,448,1024]{2,1,0:T(8,128)(2,1)}, u32[]{:S(2)}, u32[]{:S(2)}) async-start(bf16[8,448,1024]{2,1,0:T(8,128)(2,1)} %bitcast.75), calls=%async_computation.1 | async-start | bytes 14680064 | tf_op jit(solution)/shard_map/all_to_all | solution.py:66
  79.0 6.8 %slice-start = ((s8[7340032]{0:T(1024)(128)(4,1)}), s8[4194304]{0:T(1024)(128)(4,1)S(1)}, s32[]{:S(2)}) async-start(s8[7340032]{0:T(1024)(128)(4,1)} %bitcast.71), calls=%async_computation.5 | async-start | bytes 8388608
  80.5 5.4 %slice-start.1 = ((s8[7340032]{0:T(1024)(128)(4,1)}), s8[3145728]{0:T(1024)(128)(4,1)S(1)}, s32[]{:S(2)}) async-start(s8[7340032]{0:T(1024)(128)(4,1)} %bitcast.71), calls=%async_computation.6 | async-start | bytes 6291456
  139.9 87.7 %all-to-all-start.2 = ((bf16[8,448,1024]{2,1,0:T(8,128)(2,1)}), bf16[8,448,1024]{2,1,0:T(8,128)(2,1)}, u32[]{:S(2)}, u32[]{:S(2)}) async-start(bf16[8,448,1024]{2,1,0:T(8,128)(2,1)} %bitcast.74), calls=%async_computation.2 | async-start | bytes 14680064 | tf_op jit(solution)/shard_map/all_to_all | solution.py:66
  151.6 17.3 %slice-start.2 = ((bf16[3584,1024]{1,0:T(8,128)(2,1)}), bf16[3584,256]{1,0:T(8,128)(2,1)S(1)}, s32[]{:S(2)}) async-start(bf16[3584,1024]{1,0:T(8,128)(2,1)} %param.12), calls=%async_computation.7 | async-start | bytes 3670016 | tf_op jit(solution)/shard_map/slice | solution.py:89
  183.4 33.9 %collective-permute-start.3 = (f32[64,3584]{1,0:T(8,128)}, f32[64,3584]{1,0:T(8,128)S(1)}, u32[]{:S(2)}, u32[]{:S(2)}) collective-permute-start(f32[64,3584]{1,0:T(8,128)} %get-tuple-element.39), channel_id=1, source_target_pairs={{0,1},{1,2},{2,3},{3,0},{4,5},{5,6},{6,7},{7,4},{8,9},{9,10},{10,1... | collective-permute-start | bytes 2752520 | tf_op jit(solution)/shard_map/ppermute | solution.py:30
  184.7 41.8 %collective-permute-start.4 = (f32[64,3584]{1,0:T(8,128)}, f32[64,3584]{1,0:T(8,128)S(1)}, u32[]{:S(2)}, u32[]{:S(2)}) collective-permute-start(f32[64,3584]{1,0:T(8,128)} %get-tuple-element.38), channel_id=1, source_target_pairs={{0,3},{1,0},{2,1},{3,2},{4,7},{5,4},{6,5},{7,6},{8,11},{9,8},{10,9... | collective-permute-start | bytes 2752520 | tf_op jit(solution)/shard_map/ppermute | solution.py:30
  217.4 39.1 %copy-start = (f32[64,3584]{1,0:T(8,128)}, f32[64,3584]{1,0:T(8,128)S(1)}, u32[]{:S(2)}) copy-start(f32[64,3584]{1,0:T(8,128)S(1)} %collective-permute-done.3) | copy-start | bytes 2752516
  226.5 29.9 %copy-start.1 = (f32[64,3584]{1,0:T(8,128)}, f32[64,3584]{1,0:T(8,128)S(1)}, u32[]{:S(2)}) copy-start(f32[64,3584]{1,0:T(8,128)S(1)} %collective-permute-done.4) | copy-start | bytes 2752516
  227.6 67.8 %all-to-all-start.4 = ((bf16[8,448,768]{2,1,0:T(8,128)(2,1)}), bf16[8,448,768]{2,1,0:T(8,128)(2,1)}, u32[]{:S(2)}, u32[]{:S(2)}) async-start(bf16[8,448,768]{2,1,0:T(8,128)(2,1)} %bitcast.76), calls=%async_computation.4 | async-start | bytes 11010048 | tf_op jit(solution)/shard_map/all_to_all | solution.py:66
  233.7 42.3 %collective-permute-start.5 = (f32[64,3584]{1,0:T(8,128)}, f32[64,3584]{1,0:T(8,128)}, u32[]{:S(2)}, u32[]{:S(2)}) collective-permute-start(f32[64,3584]{1,0:T(8,128)} %get-tuple-element.36), channel_id=1, source_target_pairs={{0,2},{1,3},{2,0},{3,1},{4,6},{5,7},{6,4},{7,5},{8,10},{9,11},{10,... | collective-permute-start | bytes 2752520 | tf_op jit(solution)/shard_map/ppermute | solution.py:30
  295.4 35.0 %all-to-all-start.3 = ((bf16[8,448,256]{2,1,0:T(8,128)(2,1)}), bf16[8,448,256]{2,1,0:T(8,128)(2,1)S(1)}, u32[]{:S(2)}, u32[]{:S(2)}) async-start(bf16[8,448,256]{2,1,0:T(8,128)(2,1)} %bitcast.79), calls=%async_computation.3 | async-start | bytes 3670016 | tf_op jit(solution)/shard_map/all_to_all | solution.py:66

commit v3 on v2

--- a/solution.py
+++ b/solution.py
@@ -5,20 +5,6 @@
 
 D = 4096
 A_DEV = 32
-
-
-def rows_gather(window):
-    peers = lax.axis_size("rows")
-    me = lax.axis_index("rows")
-    held = window[:, :, None]
-    reach = peers // 2
-    while reach >= 1:
-        other = lax.ppermute(held, "rows", [(r, r ^ reach) for r in range(peers)])
-        upper = (me // reach) % 2 == 1
-        pair = jnp.stack([jnp.where(upper, other, held), jnp.where(upper, held, other)], axis=3)
-        held = pair.reshape(pair.shape[0], pair.shape[1], -1, pair.shape[4])
-        reach //= 2
-    return held
 
 
 def cols_reduce(parts):
@@ -59,6 +45,8 @@
     at_rank = (arrival_rank[None, :] == jnp.arange(capacity, dtype=jnp.int32)[:, None]).astype(jnp.bfloat16)
     found = jnp.einsum("hsi,ri->hsr", halves, at_rank, preferred_element_type=jnp.float32)
     wanted = found[0].astype(jnp.int32) * 256 + found[1].astype(jnp.int32)
+    wanted, up_held, gate_held = lax.optimization_barrier((wanted, up_a, gate_a))
+    window = jnp.concatenate([up_held[::stride], gate_held[::stride]], axis=0)
     asked_rows = lax.all_to_all(wanted, "rows", split_axis=0, concat_axis=0, tiled=True)
 
     def exchange(rows):
@@ -69,12 +57,14 @@
     asked = asked_rows.reshape(-1)
     slot = source * capacity + arrival_rank
 
-    pieces = rows_gather(jnp.stack([up_a[::stride], gate_a[::stride]]))
-    wide = pieces.reshape(2, A_DEV * peers, features)
-
+    asked, window = lax.optimization_barrier((asked, window))
+    sent = jnp.broadcast_to(window[None], (peers,) + window.shape)
+    pieces = lax.all_to_all(sent, "rows", split_axis=0, concat_axis=0, tiled=True)
     up_rows = pick(up_b, asked)
-    up_rows, wide = lax.optimization_barrier((up_rows, wide))
+    up_rows, pieces = lax.optimization_barrier((up_rows, pieces))
     up_moved = exchange(up_rows)
+    pieces = pieces.reshape(peers, 2, A_DEV, features)
+    wide = pieces.transpose(1, 2, 0, 3).reshape(2, A_DEV * peers, features)
 
     partial_value = jnp.einsum("kd,jd->kj", wide[0], up_b, preferred_element_type=jnp.float32)
     partial_value = partial_value + jnp.einsum(
@@ -95,17 +85,15 @@
     terms[1::2] = tied[3:]
     left = exchange(left_rows)
     gate_mean = mix(gate_a, pick(gate_moved, slot))
-    tied = lax.optimization_barrier((right_rows, gate_mean) + tuple(terms[::2]))
-    right_rows, gate_mean = tied[:2]
-    terms[::2] = tied[2:]
-    right = exchange(right_rows)
-    left_mean = mix(down_a[:, :cut], pick(left, slot))
-    down_mean = lax.dynamic_update_slice(jnp.zeros_like(down_a), left_mean, (0, 0))
     total = terms[0]
     for term in terms[1:]:
         total = total + term
     costs_out = (total * cost_scale).T
-    right, down_mean, costs_out = lax.optimization_barrier((right, down_mean, costs_out))
+    right_rows, gate_mean, costs_out = lax.optimization_barrier((right_rows, gate_mean, costs_out))
+    right = exchange(right_rows)
+    left_mean = mix(down_a[:, :cut], pick(left, slot))
+    down_mean = lax.pad(left_mean, jnp.zeros((), left_mean.dtype), ((0, 0, 0), (0, features - cut, 0)))
+    right, down_mean = lax.optimization_barrier((right, down_mean))
     right_mean = mix(down_a[:, cut:], pick(right, slot))
     down_mean = lax.dynamic_update_slice(down_mean, right_mean, (0, cut))
     return (costs_out, up_mean, gate_mean, down_mean)

time: 347 us -> 334 us (0.963)
  waiting for transfers between devices: 97.1 us -> 85.8 us
    all_to_all x4, waiting for transfers between devices: 70.6 us -> 56.9 us  [exchange(): lax.all_to_all(moved, 'rows', split_axis=0, concat_axis=0, tiled=True)]
    ppermute x3, waiting for transfers between devices: 16.7 us -> 28.9 us  [cols_reduce(): lax.ppermute(piece, 'cols', [(c, (c + shift) % count) for c in range(coun...]
    ppermute x3 -> x0, waiting for transfers between devices: 6.58 us -> none  [rows_gather(): other = lax.ppermute(held, 'rows', [(r, r ^ reach) for r in range(peers)])]
    all_to_all x0 -> x1, starting transfers between devices: none -> 4.2 us  [local(): lax.all_to_all(sent, 'rows', split_axis=0, concat_axis=0, tiled=True)]
    dynamic_update_slice x1 -> x0, local copies, waits for them, and re-layouts: 4.07 us -> none  [local(): lax.dynamic_update_slice(jnp.zeros_like(down_a), left_mean, (0, 0))]
    pad x0 -> x1, local copies, waits for them, and re-layouts: none -> 4.07 us  [local(): lax.pad(left_mean, jnp.zeros((), left_mean.dtype), ((0, 0, 0), (0, featur...]
    ppermute x3 -> x0, starting transfers between devices: 3.5 us -> none  [rows_gather(): other = lax.ppermute(held, 'rows', [(r, r ^ reach) for r in range(peers)])]
    slice x4 -> x3, local copies, waits for them, and re-layouts: 8.17 us -> 6.69 us  [the longest x2 6.39 us: local(): window = jnp.concatenate([up_held[::stride], gate_held[::stride]], axis=0)]
  transfers between devices with their start and end apart: 11 -> 9, of which waited for: 7 -> 5; matrix products, arithmetic and copies ran while one was open for 55% -> 57% of each run, Pallas kernels for 0% -> 0%
where the time goes in v3:
time: 334 us; the launch traced here: 332 us
  local copies, waits for them, and re-layouts  160 us (48%)
  waiting for transfers between devices  85.8 us (26%)
  other arithmetic  40.6 us (12%)
  starting transfers between devices  34.9 us (10%)
  matrix products  10.6 us (3%)
    gather x8, local copies, waits for them, and re-layouts, pick(): return array.at[index].get(mode='promise_in_bounds')  138 us
    all_to_all x4, waiting for transfers between devices, exchange(): lax.all_to_all(moved, 'rows', split_axis=0, concat_axis=0, tiled=True)  56.9 us
    convert_element_type x3, other arithmetic, mix(): ((initial.astype(jnp.float32) + picked.astype(jnp.float32)) * 0.5).astype...  29.9 us
    ppermute x3, waiting for transfers between devices, cols_reduce(): lax.ppermute(piece, 'cols', [(c, (c + shift) % count) for c in range(coun...  28.9 us
    all_to_all x4, starting transfers between devices, exchange(): lax.all_to_all(moved, 'rows', split_axis=0, concat_axis=0, tiled=True)  22.4 us
  transfers between devices with their start and end apart: 9, of which 5 were waited for; matrix products, arithmetic and copies ran while one was open for 57% of the time, Pallas kernels for 0%

profile of v3, /device:TPU:11, one launch (start us, length us, event | category | flops | bytes accessed | tf_op | source)
XLA Modules:
  0.0 332.3 jit_solution(16120420972539285700)
XLA Ops:
  1.4 2.3 reduce-window.6
  7.0 4.5 %all-to-all-start = ((s32[8,1,448]{2,1,0:T(1,128)}), s32[8,1,448]{2,1,0:T(1,128)S(1)}, u32[]{:S(2)}, u32[]{:S(2)}) async-start(s32[8,1,448]{2,1,0:T(1,128)} %copy.11), calls=%async_computation | async-start | bytes 32768 | tf_op jit(solution)/shard_map/all_to_all | solution.py:50
  11.5 3.2 slice.43
  14.7 3.2 slice.44
  19.2 4.2 %all-to-all-start.1 = ((bf16[8,64,1024]{2,1,0:T(8,128)(2,1)}), bf16[8,64,1024]{2,1,0:T(8,128)(2,1)S(1)}, u32[]{:S(2)}, u32[]{:S(2)}) async-start(bf16[8,64,1024]{2,1,0:T(8,128)(2,1)} %broadcast_in_dim.7), calls=%async_computation.1 | async-start | bytes 2097152 | tf_op jit(solution)/shard_map/all_to_all | solution.py:62
  23.4 20.4 %gather_fusion.2 = bf16[3584,1024]{1,0:T(8,128)(2,1)} fusion(bf16[3584,1024]{1,0:T(8,128)(2,1)} %param.10, s32[4096]{0:T(1024)S(1)} %pad_clamp_fusion.1), kind=kCustom, calls=%fused_computation.2 | custom fusion | bytes 14694400 | tf_op jit(solution)/shard_map/gather | solution.py:21
  43.8 4.8 %all-to-all-start.2 = ((bf16[8,448,1024]{2,1,0:T(8,128)(2,1)}), bf16[8,448,1024]{2,1,0:T(8,128)(2,1)}, u32[]{:S(2)}, u32[]{:S(2)}) async-start(bf16[8,448,1024]{2,1,0:T(8,128)(2,1)} %bitcast.55), calls=%async_computation.2 | async-start | bytes 14680064 | tf_op jit(solution)/shard_map/all_to_all | solution.py:54
  48.6 20.4 %gather_fusion.4 = bf16[3584,1024]{1,0:T(8,128)(2,1)} fusion(bf16[3584,1024]{1,0:T(8,128)(2,1)} %param.11, s32[4096]{0:T(1024)S(1)} %pad_clamp_fusion.1), kind=kCustom, calls=%fused_computation.4 | custom fusion | bytes 14694400 | tf_op jit(solution)/shard_map/gather | solution.py:21
  69.6 5.5 %fusion.9 = f32[256,3584]{1,0:T(8,128)S(1)} fusion(bf16[3584,1024]{1,0:T(8,128)(2,1)} %param.10, bf16[2,32,8,1024]{3,2,1,0:T(8,128)(2,1)S(1)} %bitcast.60), kind=kOutput, calls=%fused_computation.28 | convolution fusion | flops 1879048192 | bytes 11534336 | tf_op jit(solution)/shard_map/kd,jd->kj/dot_general | solution.py:69
  75.1 4.0 %convolution_add_fusion = f32[256,3584]{1,0:T(8,128)} fusion(f32[256,3584]{1,0:T(8,128)S(1)} %fusion.9, bf16[3584,1024]{1,0:T(8,128)(2,1)S(1)} %bitcast.52, bf16[2,32,8,1024]{3,2,1,0:T(8,128)(2,1)S(1)} %bitcast.61), kind=kOutput, calls=%fused_computation.14 | convolution fusion | flops 1879965696 | bytes 15204352 | tf_op jit(solution)/shard_map/kd,jd->kj/dot_general | solution.py:70
  79.1 50.8 %all-to-all-done.2 = bf16[8,448,1024]{2,1,0:T(8,128)(2,1)} async-done(((bf16[8,448,1024]{2,1,0:T(8,128)(2,1)}), bf16[8,448,1024]{2,1,0:T(8,128)(2,1)}, u32[]{:S(2)}, u32[]{:S(2)}) %all-to-all-start.2) | async-done | bytes 7340064 | tf_op jit(solution)/shard_map/all_to_all | solution.py:54
  129.9 6.3 %all-to-all-start.3 = ((bf16[8,448,1024]{2,1,0:T(8,128)(2,1)}), bf16[8,448,1024]{2,1,0:T(8,128)(2,1)}, u32[]{:S(2)}, u32[]{:S(2)}) async-start(bf16[8,448,1024]{2,1,0:T(8,128)(2,1)} %bitcast.54), calls=%async_computation.3 | async-start | bytes 14680064 | tf_op jit(solution)/shard_map/all_to_all | solution.py:54
  136.2 5.5 %slice.38 = bf16[3584,768]{1,0:T(8,128)(2,1)} slice(bf16[3584,1024]{1,0:T(8,128)(2,1)} %param.12), slice={[0:3584], [0:768]} | slice | bytes 11010048 | tf_op jit(solution)/shard_map/slice | solution.py:78
  141.7 10.9 %gather_fusion.1 = bf16[3584,256]{1,0:T(8,128)(2,1)} fusion(bf16[3584,256]{1,0:T(8,128)(2,1)S(1)} %slice-done.2, s32[4096]{0:T(1024)S(1)} %pad_clamp_fusion.1), kind=kCustom, calls=%fused_computation.1 | custom fusion | bytes 3684352 | tf_op jit(solution)/shard_map/gather | solution.py:21
  152.7 17.2 %gather_fusion = bf16[3584,768]{1,0:T(8,128)(2,1)} fusion(bf16[3584,768]{1,0:T(8,128)(2,1)} %slice.38, s32[4096]{0:T(1024)S(1)} %pad_clamp_fusion.1), kind=kCustom, calls=%fused_computation | custom fusion | bytes 11024384 | tf_op jit(solution)/shard_map/gather | solution.py:21
  169.8 3.2 dynamic-slice_bitcast_fusion
  174.5 20.4 %gather_fusion.3 = bf16[3584,1024]{1,0:T(8,128)(2,1)} fusion(bf16[3584,1024]{1,0:T(8,128)(2,1)} %bitcast.6, s32[4096]{0:T(1024)S(1)} %pad_clamp_fusion), kind=kCustom, calls=%fused_computation.3 | custom fusion | bytes 14694400 | tf_op jit(solution)/shard_map/gather | solution.py:21
  194.9 12.0 %multiply_convert_fusion.1 = bf16[3584,1024]{1,0:T(8,128)(2,1)} fusion(bf16[3584,1024]{1,0:T(8,128)(2,1)} %gather_fusion.3, bf16[3584,1024]{1,0:T(8,128)(2,1)} %param.7), kind=kLoop, calls=%fused_computation.9 | loop fusion | flops 18350080 | bytes 22020096 | tf_op jit(solution)/shard_map/convert_element_type | solution.py:25
  206.9 9.7 %collective-permute-done = f32[64,3584]{1,0:T(8,128)S(1)} collective-permute-done((f32[64,3584]{1,0:T(8,128)}, f32[64,3584]{1,0:T(8,128)S(1)}, u32[]{:S(2)}, u32[]{:S(2)}) %collective-permute-start) | collective-permute-done | bytes 917536 | tf_op jit(solution)/shard_map/ppermute | solution.py:16
  217.6 6.1 %all-to-all-start.5 = ((bf16[8,448,768]{2,1,0:T(8,128)(2,1)}), bf16[8,448,768]{2,1,0:T(8,128)(2,1)}, u32[]{:S(2)}, u32[]{:S(2)}) async-start(bf16[8,448,768]{2,1,0:T(8,128)(2,1)} %bitcast.56), calls=%async_computation.5 | async-start | bytes 11010048 | tf_op jit(solution)/shard_map/all_to_all | solution.py:54
  223.7 2.3 collective-permute-start.2
  226.0 20.4 %gather_fusion.5 = bf16[3584,1024]{1,0:T(8,128)(2,1)} fusion(bf16[3584,1024]{1,0:T(8,128)(2,1)} %bitcast.16, s32[4096]{0:T(1024)S(1)} %pad_clamp_fusion), kind=kCustom, calls=%fused_computation.5 | custom fusion | bytes 14694400 | tf_op jit(solution)/shard_map/gather | solution.py:21
  246.4 19.2 %collective-permute-done.2 = f32[64,3584]{1,0:T(8,128)} collective-permute-done((f32[64,3584]{1,0:T(8,128)S(1)}, f32[64,3584]{1,0:T(8,128)}, u32[]{:S(2)}, u32[]{:S(2)}) %collective-permute-start.2) | collective-permute-done | bytes 917536 | tf_op jit(solution)/shard_map/ppermute | solution.py:16
  265.7 2.6 fusion.8
  268.2 12.0 %multiply_convert_fusion = bf16[3584,1024]{1,0:T(8,128)(2,1)} fusion(bf16[3584,1024]{1,0:T(8,128)(2,1)} %gather_fusion.5, bf16[3584,1024]{1,0:T(8,128)(2,1)} %param.8), kind=kLoop, calls=%fused_computation.8 | loop fusion | flops 18350080 | bytes 22020096 | tf_op jit(solution)/shard_map/convert_element_type | solution.py:25
  280.3 5.1 %all-to-all-done.5 = bf16[8,448,768]{2,1,0:T(8,128)(2,1)} async-done(((bf16[8,448,768]{2,1,0:T(8,128)(2,1)}), bf16[8,448,768]{2,1,0:T(8,128)(2,1)}, u32[]{:S(2)}, u32[]{:S(2)}) %all-to-all-start.5) | async-done | bytes 5505056 | tf_op jit(solution)/shard_map/all_to_all | solution.py:54
  285.4 5.1 %all-to-all-start.4 = ((bf16[8,448,256]{2,1,0:T(8,128)(2,1)}), bf16[8,448,256]{2,1,0:T(8,128)(2,1)S(1)}, u32[]{:S(2)}, u32[]{:S(2)}) async-start(bf16[8,448,256]{2,1,0:T(8,128)(2,1)} %bitcast.59), calls=%async_computation.4 | async-start | bytes 3670016 | tf_op jit(solution)/shard_map/all_to_all | solution.py:54
  290.5 17.2 %gather_fusion.6 = bf16[3584,768]{1,0:T(8,128)(2,1)} fusion(bf16[3584,768]{1,0:T(8,128)(2,1)} %bitcast.23, s32[4096]{0:T(1024)S(1)} %pad_clamp_fusion), kind=kCustom, calls=%fused_computation.6 | custom fusion | bytes 11024384 | tf_op jit(solution)/shard_map/gather | solution.py:21
  307.7 5.9 %multiply_convert_fusion.2 = bf16[3584,768]{1,0:T(8,128)(2,1)S(1)} fusion(bf16[3584,768]{1,0:T(8,128)(2,1)} %gather_fusion.6, bf16[3584,1024]{1,0:T(8,128)(2,1)} %param.9), kind=kLoop, calls=%fused_computation.10 | loop fusion | flops 13762560 | bytes 16515072 | tf_op jit(solution)/shard_map/convert_element_type | solution.py:25
  313.5 4.1 %pad.3 = bf16[3584,1024]{1,0:T(8,128)(2,1)} pad(bf16[3584,768]{1,0:T(8,128)(2,1)S(1)} %multiply_convert_fusion.2, bf16[]{:T(256)} %constant.98.clone.1), padding=0_0x0_256 | pad | bytes 12845058 | tf_op jit(solution)/shard_map/pad | solution.py:95
  317.6 10.9 %gather_fusion.7 = bf16[3584,256]{1,0:T(8,128)(2,1)} fusion(bf16[3584,256]{1,0:T(8,128)(2,1)S(1)} %bitcast.53, s32[4096]{0:T(1024)S(1)} %pad_clamp_fusion), kind=kCustom, calls=%fused_computation.7 | custom fusion | bytes 3684352 | tf_op jit(solution)/shard_map/gather | solution.py:21
  328.5 3.8 %fusion.4 = bf16[3584,1024]{1,0:T(8,128)(2,1)} fusion(bf16[3584,1024]{1,0:T(8,128)(2,1)} %pad.3, bf16[3584,256]{1,0:T(8,128)(2,1)} %gather_fusion.7, bf16[3584,1024]{1,0:T(8,128)(2,1)} %param.9), kind=kLoop, calls=%fused_computation.17 | loop fusion | flops 4587520 | bytes 5505024 | tf_op jit(solution)/shard_map/dynamic_update_slice | solution.py:98
  (36 shorter events, 8.3 us)
Async XLA Ops:
  7.0 11.0 %all-to-all-start = ((s32[8,1,448]{2,1,0:T(1,128)}), s32[8,1,448]{2,1,0:T(1,128)S(1)}, u32[]{:S(2)}, u32[]{:S(2)}) async-start(s32[8,1,448]{2,1,0:T(1,128)} %copy.11), calls=%async_computation | async-start | bytes 32768 | tf_op jit(solution)/shard_map/all_to_all | solution.py:50
  19.2 24.6 %all-to-all-start.1 = ((bf16[8,64,1024]{2,1,0:T(8,128)(2,1)}), bf16[8,64,1024]{2,1,0:T(8,128)(2,1)S(1)}, u32[]{:S(2)}, u32[]{:S(2)}) async-start(bf16[8,64,1024]{2,1,0:T(8,128)(2,1)} %broadcast_in_dim.7), calls=%async_computation.1 | async-start | bytes 2097152 | tf_op jit(solution)/shard_map/all_to_all | solution.py:62
  43.8 86.1 %all-to-all-start.2 = ((bf16[8,448,1024]{2,1,0:T(8,128)(2,1)}), bf16[8,448,1024]{2,1,0:T(8,128)(2,1)}, u32[]{:S(2)}, u32[]{:S(2)}) async-start(bf16[8,448,1024]{2,1,0:T(8,128)(2,1)} %bitcast.55), calls=%async_computation.2 | async-start | bytes 14680064 | tf_op jit(solution)/shard_map/all_to_all | solution.py:54
  69.0 6.1 %slice-start = ((s8[7340032]{0:T(1024)(128)(4,1)}), s8[4194304]{0:T(1024)(128)(4,1)S(1)}, s32[]{:S(2)}) async-start(s8[7340032]{0:T(1024)(128)(4,1)} %bitcast.51), calls=%async_computation.6 | async-start | bytes 8388608
  69.6 5.5 %slice-start.1 = ((s8[7340032]{0:T(1024)(128)(4,1)}), s8[3145728]{0:T(1024)(128)(4,1)S(1)}, s32[]{:S(2)}) async-start(s8[7340032]{0:T(1024)(128)(4,1)} %bitcast.51), calls=%async_computation.7 | async-start | bytes 6291456
  129.9 87.7 %all-to-all-start.3 = ((bf16[8,448,1024]{2,1,0:T(8,128)(2,1)}), bf16[8,448,1024]{2,1,0:T(8,128)(2,1)}, u32[]{:S(2)}, u32[]{:S(2)}) async-start(bf16[8,448,1024]{2,1,0:T(8,128)(2,1)} %bitcast.54), calls=%async_computation.3 | async-start | bytes 14680064 | tf_op jit(solution)/shard_map/all_to_all | solution.py:54
  136.2 5.5 %slice-start.2 = ((bf16[3584,1024]{1,0:T(8,128)(2,1)}), bf16[3584,256]{1,0:T(8,128)(2,1)S(1)}, s32[]{:S(2)}) async-start(bf16[3584,1024]{1,0:T(8,128)(2,1)} %param.12), calls=%async_computation.8 | async-start | bytes 3670016 | tf_op jit(solution)/shard_map/slice | solution.py:79
  173.0 33.9 %collective-permute-start.1 = (f32[64,3584]{1,0:T(8,128)}, f32[64,3584]{1,0:T(8,128)S(1)}, u32[]{:S(2)}, u32[]{:S(2)}) collective-permute-start(f32[64,3584]{1,0:T(8,128)} %get-tuple-element.43), channel_id=1, source_target_pairs={{0,3},{1,0},{2,1},{3,2},{4,7},{5,4},{6,5},{7,6},{8,11},{9,8},{10,9... | collective-permute-start | bytes 2752520 | tf_op jit(solution)/shard_map/ppermute | solution.py:16
  173.2 43.4 %collective-permute-start = (f32[64,3584]{1,0:T(8,128)}, f32[64,3584]{1,0:T(8,128)S(1)}, u32[]{:S(2)}, u32[]{:S(2)}) collective-permute-start(f32[64,3584]{1,0:T(8,128)} %get-tuple-element.44), channel_id=1, source_target_pairs={{0,1},{1,2},{2,3},{3,0},{4,5},{5,6},{6,7},{7,4},{8,9},{9,10},{10,1... | collective-permute-start | bytes 2752520 | tf_op jit(solution)/shard_map/ppermute | solution.py:16
  217.6 67.8 %all-to-all-start.5 = ((bf16[8,448,768]{2,1,0:T(8,128)(2,1)}), bf16[8,448,768]{2,1,0:T(8,128)(2,1)}, u32[]{:S(2)}, u32[]{:S(2)}) async-start(bf16[8,448,768]{2,1,0:T(8,128)(2,1)} %bitcast.56), calls=%async_computation.5 | async-start | bytes 11010048 | tf_op jit(solution)/shard_map/all_to_all | solution.py:54
  223.7 41.9 %collective-permute-start.2 = (f32[64,3584]{1,0:T(8,128)S(1)}, f32[64,3584]{1,0:T(8,128)}, u32[]{:S(2)}, u32[]{:S(2)}) collective-permute-start(f32[64,3584]{1,0:T(8,128)S(1)} %get-tuple-element.42), channel_id=1, source_target_pairs={{0,2},{1,3},{2,0},{3,1},{4,6},{5,7},{6,4},{7,5},{8,10},{9,11},{10,... | collective-permute-start | bytes 2752520 | tf_op jit(solution)/shard_map/ppermute | solution.py:16
  285.4 32.2 %all-to-all-start.4 = ((bf16[8,448,256]{2,1,0:T(8,128)(2,1)}), bf16[8,448,256]{2,1,0:T(8,128)(2,1)S(1)}, u32[]{:S(2)}, u32[]{:S(2)}) async-start(bf16[8,448,256]{2,1,0:T(8,128)(2,1)} %bitcast.59), calls=%async_computation.4 | async-start | bytes 3670016 | tf_op jit(solution)/shard_map/all_to_all | solution.py:54
